TPU v7x, 256 devices: a whole 4x4x8 slice. The times are simulated.
256 devices in a mesh: pix: 64 (over z, y, core), chan: 4 (over x).
Axes of the slice: x: 4, y: 4, z: 8, core: 2. Of those that a mesh axis runs over, the one named last changes fastest.
Arguments:
- spectra: bfloat16 [262144, 2048], P('pix', 'chan'), may hold values from 0.05 to 2100, as said below
- start: bfloat16 [64, 2048], P(None, 'chan'), may hold values from -6 to 6
- anchors: int32 [16], replicated, may hold values from 0 to 262143, as said below
Outputs:
- scores: float32 [64, 262144], P(None, 'pix')
- abundance: float32 [16, 262144], P(None, 'pix')
Inputs may be any that keep to these rules, and one draw needn't show every extreme that they name: `spectra`: every entry is positive. `anchors`: the 16 indices are distinct; pixel 0 and pixel 262144 - 1 are among them.
All inputs are finite; a program needn't handle non-finite values.
Results may differ from a plain program's by a relative error of at most 0.035.
Values may be sent and summed in bfloat16 or wider, within the bound.
No kernel may reach another device: no remote copies, remote signals or barrier semaphores. Data moves between devices by JAX's collectives and lax.ppermute only.
A program may use at most 64 MiB of HBM per device.

v0:
```python
import jax
import jax.numpy as jnp
from jax import lax
from jax.sharding import PartitionSpec as P

ITERS = 5


def tri_solve(lower, rhs):
    return lax.linalg.triangular_solve(lower, rhs, left_side=True, lower=True)


def project(loadings, weighted):
    return lax.dot_general(
        loadings, weighted, (((1,), (1,)), ((), ())), preferred_element_type=jnp.float32
    )


def local(spectra, start, anchors):
    pix_rows = spectra.shape[0]
    col_part = jnp.sum(spectra, axis=0, dtype=jnp.float32)
    colsum = lax.psum(col_part, "pix")
    row_part = jnp.sum(spectra, axis=1, dtype=jnp.float32)
    rowsum, total = lax.psum((row_part, jnp.sum(colsum)), "chan")
    expect = rowsum[:, None] * colsum[None, :] / total
    weighted = ((spectra.astype(jnp.float32) - expect) * lax.rsqrt(expect)).astype(jnp.bfloat16)
    loadings = start
    for step in range(ITERS):
        partial_proj = project(loadings, weighted).astype(jnp.bfloat16)
        proj = lax.psum(partial_proj, "chan").astype(jnp.float32).astype(jnp.bfloat16)
        back = jnp.dot(proj, weighted, preferred_element_type=jnp.float32)
        full = lax.psum(back, "pix")
        gram = lax.psum(jnp.dot(full, full.T, precision=lax.Precision.HIGHEST), "chan")
        lower = jnp.linalg.cholesky(gram)
        renewed = tri_solve(lower, full)
        loadings = renewed.astype(jnp.bfloat16)
    score_part = project(loadings, weighted)
    scores = lax.psum(score_part.astype(jnp.bfloat16), "chan").astype(jnp.float32)
    offset = lax.axis_index("pix") * pix_rows
    positions = lax.broadcasted_iota(jnp.int32, (anchors.shape[0], pix_rows), 1)
    picks = (anchors[:, None] - offset == positions).astype(jnp.float32)
    contract = (((1,), (1,)), ((), ()))
    local_rows = lax.dot_general(picks, scores, contract, precision=lax.Precision.HIGHEST)
    rows = lax.psum(local_rows, "pix")
    small = jnp.dot(rows, rows.T, precision=lax.Precision.HIGHEST)
    lower = jnp.linalg.cholesky(small)
    rhs = jnp.dot(rows, scores, precision=lax.Precision.HIGHEST)
    middle = tri_solve(lower, rhs)
    abundance = lax.linalg.triangular_solve(
        lower, middle, left_side=True, lower=True, transpose_a=True
    )
    return (scores, abundance)


def solution(mesh):
    placed = (P("pix", "chan"), P(None, "chan"), P())
    return jax.shard_map(
        local,
        mesh=mesh,
        in_specs=placed,
        out_specs=(P(None, "pix"), P(None, "pix")),
        check_vma=False,
    )
```

profile of v0, /device:TPU:8, one launch (start us, length us, event | category | flops | bytes accessed | tf_op | source)
XLA Modules:
  0.0 1646.2 jit_solution(1855062621871355629)
XLA Ops:
  10.8 126.7 %psum.141 = f32[512]{0:T(512)S(1)} all-reduce(f32[512]{0:T(512)S(1)} %get-tuple-element.5), channel_id=1, replica_groups=mesh['pix'=64,'chan'=4] {'pix'}, use_global_device_ids=true, to_apply=%region_3.0 | all-reduce | flops 512 | bytes 4096 | tf_op jit(solution)/shard_map/psum | solution.py:22
  138.0 18.1 %all-reduce = (f32[]{:T(128)}, f32[4096]{0:T(1024)S(1)}) all-reduce(f32[]{:T(128)} %reduce_sum.29, f32[4096]{0:T(1024)S(1)} %get-tuple-element.4), channel_id=1, replica_groups=mesh['pix'=64,'chan'=4] {'chan'}, use_global_device_ids=true, to_apply=%region_5.0 | all-reduce | flops 4097 | bytes 32776 | tf_op jit(solution)/shard_map/psum | solution.py:24
  164.5 48.5 %all-reduce.13.cloned.1.call-done = bf16[64,4096]{0,1:T(8,128)(2,1)} async-done(((bf16[64,4096]{0,1:T(8,128)(2,1)}), bf16[64,4096]{0,1:T(8,128)(2,1)}) %all-reduce.13.cloned.1.call-update) | async-done | bytes 524304 | tf_op jit(solution)/shard_map/psum | solution.py:30
  217.2 173.2 %all-reduce.15.cloned.1.call-done = f32[64,512]{1,0:T(8,128)} async-done(((f32[64,512]{1,0:T(8,128)}), f32[64,512]{1,0:T(8,128)}) %all-reduce.15.cloned.1.call-update) | async-done | bytes 131088 | tf_op jit(solution)/shard_map/psum | solution.py:32
  391.7 17.0 %psum.145 = f32[64,64]{0,1:T(8,128)S(1)} all-reduce(f32[64,64]{0,1:T(8,128)S(1)} %fusion.35), channel_id=1, replica_groups=mesh['pix'=64,'chan'=4] {'chan'}, use_global_device_ids=true, to_apply=%region_8.0 | all-reduce | flops 4096 | bytes 32768 | tf_op jit(solution)/shard_map/psum | solution.py:33
  408.8 5.8 cholesky.124
  426.5 45.2 %all-reduce.17.cloned.1.call-done = bf16[64,4096]{1,0:T(8,128)(2,1)} async-done(((bf16[64,4096]{1,0:T(8,128)(2,1)}), bf16[64,4096]{1,0:T(8,128)(2,1)}) %all-reduce.17.cloned.1.call-update) | async-done | bytes 524304 | tf_op jit(solution)/shard_map/psum | solution.py:30
  475.7 173.0 %all-reduce.19.cloned.1.call-done = f32[64,512]{1,0:T(8,128)} async-done(((f32[64,512]{1,0:T(8,128)}), f32[64,512]{1,0:T(8,128)}) %all-reduce.19.cloned.1.call-update) | async-done | bytes 131088 | tf_op jit(solution)/shard_map/psum | solution.py:32
  650.0 17.0 %psum.148 = f32[64,64]{0,1:T(8,128)S(1)} all-reduce(f32[64,64]{0,1:T(8,128)S(1)} %fusion.37), channel_id=1, replica_groups=mesh['pix'=64,'chan'=4] {'chan'}, use_global_device_ids=true, to_apply=%region_13.16 | all-reduce | flops 4096 | bytes 32768 | tf_op jit(solution)/shard_map/psum | solution.py:33
  667.1 5.8 cholesky.135
  684.8 45.2 %all-reduce.21.cloned.1.call-done = bf16[64,4096]{1,0:T(8,128)(2,1)} async-done(((bf16[64,4096]{1,0:T(8,128)(2,1)}), bf16[64,4096]{1,0:T(8,128)(2,1)}) %all-reduce.21.cloned.1.call-update) | async-done | bytes 524304 | tf_op jit(solution)/shard_map/psum | solution.py:30
  734.2 172.9 %all-reduce.23.cloned.1.call-done = f32[64,512]{1,0:T(8,128)} async-done(((f32[64,512]{1,0:T(8,128)}), f32[64,512]{1,0:T(8,128)}) %all-reduce.23.cloned.1.call-update) | async-done | bytes 131088 | tf_op jit(solution)/shard_map/psum | solution.py:32
  908.3 17.0 %psum.151 = f32[64,64]{0,1:T(8,128)S(1)} all-reduce(f32[64,64]{0,1:T(8,128)S(1)} %fusion.39), channel_id=1, replica_groups=mesh['pix'=64,'chan'=4] {'chan'}, use_global_device_ids=true, to_apply=%region_16.19 | all-reduce | flops 4096 | bytes 32768 | tf_op jit(solution)/shard_map/psum | solution.py:33
  925.4 5.8 cholesky.146
  943.2 45.2 %all-reduce.25.cloned.1.call-done = bf16[64,4096]{1,0:T(8,128)(2,1)} async-done(((bf16[64,4096]{1,0:T(8,128)(2,1)}), bf16[64,4096]{1,0:T(8,128)(2,1)}) %all-reduce.25.cloned.1.call-update) | async-done | bytes 524304 | tf_op jit(solution)/shard_map/psum | solution.py:30
  992.3 173.2 %all-reduce.27.cloned.1.call-done = f32[64,512]{1,0:T(8,128)} async-done(((f32[64,512]{1,0:T(8,128)}), f32[64,512]{1,0:T(8,128)}) %all-reduce.27.cloned.1.call-update) | async-done | bytes 131088 | tf_op jit(solution)/shard_map/psum | solution.py:32
  1166.7 17.0 %psum.154 = f32[64,64]{0,1:T(8,128)S(1)} all-reduce(f32[64,64]{0,1:T(8,128)S(1)} %fusion.41), channel_id=1, replica_groups=mesh['pix'=64,'chan'=4] {'chan'}, use_global_device_ids=true, to_apply=%region_19.22 | all-reduce | flops 4096 | bytes 32768 | tf_op jit(solution)/shard_map/psum | solution.py:33
  1183.8 5.8 cholesky.157
  1201.6 45.2 %all-reduce.29.cloned.1.call-done = bf16[64,4096]{1,0:T(8,128)(2,1)} async-done(((bf16[64,4096]{1,0:T(8,128)(2,1)}), bf16[64,4096]{1,0:T(8,128)(2,1)}) %all-reduce.29.cloned.1.call-update) | async-done | bytes 524304 | tf_op jit(solution)/shard_map/psum | solution.py:30
  1250.8 173.0 %all-reduce.31.cloned.1.call-done = f32[64,512]{1,0:T(8,128)} async-done(((f32[64,512]{1,0:T(8,128)}), f32[64,512]{1,0:T(8,128)}) %all-reduce.31.cloned.1.call-update) | async-done | bytes 131088 | tf_op jit(solution)/shard_map/psum | solution.py:32
  1425.1 17.0 %psum.157 = f32[64,64]{0,1:T(8,128)S(1)} all-reduce(f32[64,64]{0,1:T(8,128)S(1)} %fusion.43), channel_id=1, replica_groups=mesh['pix'=64,'chan'=4] {'chan'}, use_global_device_ids=true, to_apply=%region_22.25 | all-reduce | flops 4096 | bytes 32768 | tf_op jit(solution)/shard_map/psum | solution.py:33
  1442.2 5.8 cholesky.168
  1459.9 45.3 %all-reduce.33.cloned.1.call-done = bf16[64,4096]{1,0:T(8,128)(2,1)} async-done(((bf16[64,4096]{1,0:T(8,128)(2,1)}), bf16[64,4096]{1,0:T(8,128)(2,1)}) %all-reduce.33.cloned.1.call-update) | async-done | bytes 524304 | tf_op jit(solution)/shard_map/psum | solution.py:38
  1506.5 123.9 %psum.159 = f32[16,64]{1,0:T(8,128)S(1)} all-reduce(f32[16,64]{1,0:T(8,128)S(1)} %fusion.3), channel_id=1, replica_groups=mesh['pix'=64,'chan'=4] {'pix'}, use_global_device_ids=true, to_apply=%region_24.27 | all-reduce | flops 1024 | bytes 8192 | tf_op jit(solution)/shard_map/psum | solution.py:44
  (96 shorter events, 108.9 us)
Async XLA Ops:
  7.2 155.1 %copy-start = (bf16[64,512]{1,0:T(8,128)(2,1)S(1)}, bf16[64,512]{1,0:T(8,128)(2,1)}, u32[]{:S(2)}) copy-start(bf16[64,512]{1,0:T(8,128)(2,1)} %param.7) | copy-start | bytes 196612
  7.2 205.9 %all-reduce.13.cloned.1.call-start = ((), (), s32[]{:S(2)}) async-start(), calls=%async_computation | async-start | bytes 2097152 | tf_op jit(solution)/shard_map/psum | solution.py:30
  160.3 1.9 copy-start.1
  164.5 225.9 %all-reduce.15.cloned.1.call-start = ((), (), s32[]{:S(2)}) async-start(), calls=%async_computation.1 | async-start | bytes 262144 | tf_op jit(solution)/shard_map/psum | solution.py:32
  217.1 254.6 %all-reduce.17.cloned.1.call-start = ((), (), s32[]{:S(2)}) async-start(), calls=%async_computation.2 | async-start | bytes 1048576 | tf_op jit(solution)/shard_map/psum | solution.py:30
  426.5 222.3 %all-reduce.19.cloned.1.call-start = ((), (), s32[]{:S(2)}) async-start(), calls=%async_computation.3 | async-start | bytes 262144 | tf_op jit(solution)/shard_map/psum | solution.py:32
  475.6 254.4 %all-reduce.21.cloned.1.call-start = ((), (), s32[]{:S(2)}) async-start(), calls=%async_computation.4 | async-start | bytes 1048576 | tf_op jit(solution)/shard_map/psum | solution.py:30
  684.8 222.3 %all-reduce.23.cloned.1.call-start = ((), (), s32[]{:S(2)}) async-start(), calls=%async_computation.5 | async-start | bytes 262144 | tf_op jit(solution)/shard_map/psum | solution.py:32
  733.9 254.4 %all-reduce.25.cloned.1.call-start = ((), (), s32[]{:S(2)}) async-start(), calls=%async_computation.6 | async-start | bytes 1048576 | tf_op jit(solution)/shard_map/psum | solution.py:30
  943.1 222.4 %all-reduce.27.cloned.1.call-start = ((), (), s32[]{:S(2)}) async-start(), calls=%async_computation.7 | async-start | bytes 262144 | tf_op jit(solution)/shard_map/psum | solution.py:32
  992.3 254.6 %all-reduce.29.cloned.1.call-start = ((), (), s32[]{:S(2)}) async-start(), calls=%async_computation.8 | async-start | bytes 1048576 | tf_op jit(solution)/shard_map/psum | solution.py:30
  1201.6 222.2 %all-reduce.31.cloned.1.call-start = ((), (), s32[]{:S(2)}) async-start(), calls=%async_computation.9 | async-start | bytes 262144 | tf_op jit(solution)/shard_map/psum | solution.py:32
  1250.7 209.2 %copy-start.2 = (s32[16]{0:T(128)S(1)}, s32[16]{0:T(128)}, u32[]{:S(2)}) copy-start(s32[16]{0:T(128)} %param.8) | copy-start | bytes 196
  1250.7 254.4 %all-reduce.33.cloned.1.call-start = ((), (), s32[]{:S(2)}) async-start(), calls=%async_computation.10 | async-start | bytes 1048576 | tf_op jit(solution)/shard_map/psum | solution.py:38
Sparse Core Ops, SparseCore 0:
  164.6 48.4 all-reduce.12
  217.5 172.8 all-reduce.14
  426.6 45.1 all-reduce.16
  476.1 172.6 all-reduce.18
  684.9 45.1 all-reduce.20
  734.4 172.6 all-reduce.22
  943.2 45.1 all-reduce.24
  992.8 172.6 all-reduce.26
  1201.7 45.1 all-reduce.28
  1251.1 172.6 all-reduce.30
  1460.0 45.1 all-reduce.32
where the time goes:
time: 1650 us
  waiting for transfers between devices  1140 us (69%)
  blocking collectives  354 us (21%)
  other arithmetic  74.8 us (5%)
  matrix products  60.2 us (4%)
    psum x5, waiting for transfers between devices, local(): full = lax.psum(back, 'pix')  865 us
    psum x5, waiting for transfers between devices, local(): lax.psum(partial_proj, 'chan').astype(jnp.float32).astype(jnp.bfloat16)  229 us
    psum x1, blocking collectives, local(): colsum = lax.psum(col_part, 'pix')  127 us
    psum x1, blocking collectives, local(): rows = lax.psum(local_rows, 'pix')  124 us
    psum x5, blocking collectives, local(): lax.psum(jnp.dot(full, full.T, precision=lax.Precision.HIGHEST), 'chan')  85 us
    psum x1, waiting for transfers between devices, local(): lax.psum(score_part.astype(jnp.bfloat16), 'chan').astype(jnp.float32)  45.3 us
  transfers between devices with their start and end apart: 11, of which 11 were waited for; matrix products, arithmetic and copies ran while one was open for 0% of the time, Pallas kernels for 0%

commit v1 on v0

v1 whole, which is shorter than its diff:
```python
import jax
import jax.numpy as jnp
from jax import lax
from jax.sharding import Mesh, PartitionSpec as P

ITERS = 5
NZ, NY, NC, NX = 8, 4, 2, 4
F32, BF16 = jnp.float32, jnp.bfloat16
HIGHEST = lax.Precision.HIGHEST


def tri_solve(lower, rhs, **kw):
    return lax.linalg.triangular_solve(lower, rhs, left_side=True, lower=True, **kw)


def ring(n, step):
    return [(i, (i + step) % n) for i in range(n)]


def from_x(v, d):
    return lax.ppermute(v, "x", ring(NX, -d))


def tn(a, b):
    return lax.dot_general(a, b, (((0,), (0,)), ((), ())), preferred_element_type=F32)


def nt(a, b, **kw):
    return lax.dot_general(a, b, (((1,), (1,)), ((), ())), preferred_element_type=F32, **kw)


def pair_sum(a, b, c, d):
    return (a + b) + (c + d)


def weigh(block, rowsum, colsum, total):
    expect = rowsum[:, None] * colsum[None, :] / total
    return ((block.astype(F32) - expect) * lax.rsqrt(expect)).astype(BF16)


def in_order(parts, me):
    n = len(parts)
    twice = jnp.stack(parts + parts[:-1])
    return lax.dynamic_slice_in_dim(twice, (n - me) % n, n, 0)


def local(spectra, start, anchors):
    pix, grp = spectra.shape
    k = start.shape[0]
    na = anchors.shape[0]
    x, core, y, z = (lax.axis_index(a) for a in ("x", "core", "y", "z"))
    quart = pix // NX

    def quarter(v, j):
        return lax.dynamic_slice_in_dim(v, ((j + 2 * NX) % NX) * quart, quart, 0)

    first = core == 0
    up_a = lax.ppermute(quarter(spectra, x - 2), "x", ring(NX, -1))
    dn_a = lax.ppermute(quarter(spectra, x), "x", ring(NX, 1))
    up_b = lax.ppermute(quarter(spectra, x - 1), "x", ring(NX, -1))
    dn_b = lax.ppermute(quarter(spectra, x + 1), "x", ring(NX, 1))
    pairs = [(i, (i - 1) % NX) for i in range(NX)] + [(NX + i, NX + (i + 1) % NX) for i in range(NX)]
    extra = lax.ppermute(quarter(spectra, jnp.where(first, x + 1, x + 2)), ("core", "x"), pairs)

    col_part = jnp.sum(spectra, axis=0, dtype=F32)
    row_part = jnp.sum(spectra, axis=1, dtype=F32)
    rowsum = pair_sum(row_part, from_x(row_part, 2), from_x(row_part, 1), from_x(row_part, 3))
    npix = NZ * NY * NC
    every = lax.all_to_all(jnp.broadcast_to(col_part[None], (npix, grp)), ("z", "y", "core"), 0, 0, tiled=True)
    col = [jnp.sum(every, axis=0)]
    col += [from_x(col[0], d) for d in (1, 2, 3)]
    sums = [jnp.sum(v) for v in col]
    total = pair_sum(sums[0], sums[2], sums[1], sums[3])

    w = weigh(spectra, rowsum, col[0], total)
    quarter_rows = lambda j: quarter(rowsum, j)
    w_up = weigh(jnp.concatenate([up_a, up_b]), jnp.concatenate([quarter_rows(x - 1), quarter_rows(x)]), col[1], total)
    w_dn = weigh(jnp.concatenate([dn_a, dn_b]), jnp.concatenate([quarter_rows(x - 1), quarter_rows(x)]), col[3], total)
    j_extra = jnp.where(first, x - 2, x + 1)
    w_ex = weigh(extra, quarter_rows(j_extra), jnp.where(first, col[1], col[3]), total)

    own_a, own_b, own_ex = quarter(w, x - 1), quarter(w, x), quarter(w, j_extra)
    g_own = tn(w, w)
    g_up = tn(own_a, w_up[:quart])
    g_dn = tn(w_dn, jnp.concatenate([own_a, own_b]))
    swap = (x == 0) | (x == 3)
    g_op = tn(jnp.where(swap, w_up, w_dn), jnp.where(swap, w_dn, w_up))
    g_ex = tn(jnp.where(first, own_ex, w_ex), jnp.where(first, w_ex, own_ex))
    g_up = g_up + jnp.where(first, g_ex, 0.0)
    g_dn = g_dn + jnp.where(first, 0.0, g_ex)
    g = jnp.stack([g_own, g_up, g_dn, g_op])

    offset = ((z * NY + y) * NC + core) * pix
    positions = lax.broadcasted_iota(jnp.int32, (na, pix), 1)
    picks = (anchors[:, None] - offset == positions).astype(BF16)
    picked = jnp.dot(picks, w, preferred_element_type=F32)
    share = lax.all_to_all(picked.reshape(npix, na * grp // npix), ("z", "y", "core"), 0, 0, tiled=True)
    share = jnp.sum(share, axis=0)
    held = lax.all_to_all(jnp.broadcast_to(share[None], (npix, share.shape[0])), ("z", "y", "core"), 0, 0, tiled=True)
    anchor_w = held.reshape(na, grp).astype(BF16)
    anchor_ws = [anchor_w] + [from_x(anchor_w, d) for d in (1, 2, 3)]

    n1, n2, n3 = grp // NC, grp // NC // NY, grp // npix
    take = lambda v, i, n: lax.dynamic_slice_in_dim(v, i * n, n, 1)
    g = take(g, core, n1) + lax.ppermute(take(g, 1 - core, n1), "core", ring(NC, 1))
    sent = [lax.ppermute(take(g, (y + d) % NY, n2), "y", ring(NY, d)) for d in (1, 2, 3)]
    g = take(g, y, n2) + sent[0] + sent[1] + sent[2]
    g = g.reshape(4, NZ, n3, grp).transpose(1, 0, 2, 3)
    g = jnp.sum(lax.all_to_all(g, "z", 0, 0, tiled=True), axis=0)
    below = lax.ppermute(jnp.stack([g[1], g[3]]), "x", ring(NX, 1))
    above = lax.ppermute(jnp.stack([g[2], g[3]]), "x", ring(NX, -1))
    g = jnp.stack([g[0], g[1] + above[0], g[2] + below[0], below[1] + above[1]])
    g = lax.all_to_all(jnp.broadcast_to(g[None], (NZ,) + g.shape), "z", 0, 0, tiled=True)
    g = in_order([g] + [lax.ppermute(g, "y", ring(NY, -d)) for d in (1, 2, 3)], y)
    g = in_order([g, lax.ppermute(g, "core", ring(NC, 1))], core)
    g = g.transpose(3, 0, 1, 2, 4, 5).reshape(4, grp, grp)
    opposite = jnp.where(x < 2, g[3].T, g[3])
    g = jnp.concatenate([g[0], g[1].T, opposite, g[2]])
    rounded = lax.reduce_precision(g, 8, 7)
    g_hi, g_lo = rounded.astype(BF16), (g - rounded).astype(BF16)

    loads = [start] + [from_x(start, d) for d in (1, 2, 3)]
    for step in range(ITERS):
        whole = jnp.concatenate(loads, axis=1)
        back = jnp.dot(whole, g_hi, preferred_element_type=F32) + jnp.dot(whole, g_lo, preferred_element_type=F32)
        backs = [back] + [from_x(back, d) for d in (1, 2, 3)]
        grams = [nt(b, b, precision=HIGHEST) for b in backs]
        gram = pair_sum(grams[0], grams[2], grams[1], grams[3])
        lower = jnp.linalg.cholesky(gram)
        loads = [v.astype(BF16) for v in jnp.split(tri_solve(lower, jnp.concatenate(backs, axis=1)), 4, axis=1)]

    part = nt(loads[0], w).astype(BF16)
    take = lambda v, i: lax.dynamic_slice_in_dim(v, (i % NX) * quart, quart, 1)
    sent = [lax.ppermute(take(part, x + d), "x", ring(NX, d)) for d in (1, 2, 3)]
    mine = sum(v.astype(F32) for v in [take(part, x)] + sent).astype(BF16)
    scores = in_order([mine] + [from_x(mine, d) for d in (1, 2, 3)], x)
    scores = scores.transpose(1, 0, 2).reshape(k, pix).astype(F32)
    rows = [nt(a, b) for a, b in zip(anchor_ws, loads)]
    rows = pair_sum(rows[0], rows[2], rows[1], rows[3])
    small = nt(rows, rows, precision=HIGHEST)
    lower = jnp.linalg.cholesky(small)
    mix = tri_solve(lower, tri_solve(lower, rows), transpose_a=True)
    abundance = jnp.dot(mix, scores, precision=HIGHEST)
    return (scores, abundance)


def solution(mesh):
    fine = Mesh(mesh.devices.reshape(NZ, NY, NC, NX), ("z", "y", "core", "x"))
    pix = ("z", "y", "core")
    return jax.shard_map(
        local,
        mesh=fine,
        in_specs=(P(pix, "x"), P(None, "x"), P()),
        out_specs=(P(None, pix), P(None, pix)),
        check_vma=False,
    )
```

time: 1650 us -> 462 us (0.28)
  waiting for transfers between devices: 1140 us -> 165 us
  blocking collectives: 354 us -> 39.7 us
  starting transfers between devices: 0.64 us -> 94.5 us
  local copies, waits for them, and re-layouts: 2.38 us -> 20.3 us
  matrix products: 60.2 us -> 43.2 us
    psum x11 -> x0, waiting for transfers between devices: 1140 us -> none  [the longest x5 865 us: local(): full = lax.psum(back, 'pix')]
    psum x8 -> x0, blocking collectives: 354 us -> none  [the longest x1 127 us: local(): colsum = lax.psum(col_part, 'pix')]
    ppermute x0 -> x48, waiting for transfers between devices: none -> 139 us  [the longest x30 73.5 us: from_x(): return lax.ppermute(v, 'x', ring(NX, -d))]
    ppermute x0 -> x48, starting transfers between devices: none -> 69.6 us  [the longest x30 48.8 us: from_x(): return lax.ppermute(v, 'x', ring(NX, -d))]
    all_to_all x0 -> x2, blocking collectives: none -> 39.7 us  [the longest x1 23.8 us: local(): g = jnp.sum(lax.all_to_all(g, 'z', 0, 0, tiled=True), axis=0)]
    all_to_all x0 -> x3, waiting for transfers between devices: none -> 26 us  [the longest x1 8.88 us: local(): lax.all_to_all(jnp.broadcast_to(col_part[None], (npix, grp)), ('z', 'y',...]
    all_to_all x0 -> x3, starting transfers between devices: none -> 24.9 us  [the longest x1 12.1 us: local(): lax.all_to_all(jnp.broadcast_to(col_part[None], (npix, grp)), ('z', 'y',...]
    dot_general x19 -> x43, matrix products: 52.5 us -> 39.7 us  [the longest x5 15.3 us: tn(): lax.dot_general(a, b, (((0,), (0,)), ((), ())), preferred_element_type=F32)]
  transfers between devices with their start and end apart: 11 -> 51, of which waited for: 11 -> 34; matrix products, arithmetic and copies ran while one was open for 0% -> 26% of each run, Pallas kernels for 0% -> 0%
where the time goes in v1:
time: 462 us; the launch traced here: 453 us
  waiting for transfers between devices  165 us (36%)
  starting transfers between devices  94.5 us (20%)
  other arithmetic  86 us (19%)
  matrix products  43.2 us (9%)
  blocking collectives  39.7 us (9%)
  local copies, waits for them, and re-layouts  20.3 us (4%)
    ppermute x30, waiting for transfers between devices, from_x(): return lax.ppermute(v, 'x', ring(NX, -d))  73.5 us
    ppermute x30, starting transfers between devices, from_x(): return lax.ppermute(v, 'x', ring(NX, -d))  48.8 us
    another operation x15, other arithmetic, local(): lower = jnp.linalg.cholesky(gram)  32.6 us
    another operation x12, other arithmetic, tri_solve(): lax.linalg.triangular_solve(lower, rhs, left_side=True, lower=True, **kw)  29.6 us
    all_to_all x1, blocking collectives, local(): g = jnp.sum(lax.all_to_all(g, 'z', 0, 0, tiled=True), axis=0)  23.8 us
    ppermute x3, waiting for transfers between devices, local(): lax.ppermute(take(g, (y + d) % NY, n2), 'y', ring(NY, d))  22.4 us
    ppermute x3, waiting for transfers between devices, local(): lax.ppermute(g, 'y', ring(NY, -d))  16.1 us
    all_to_all x1, blocking collectives, local(): lax.all_to_all(jnp.broadcast_to(g[None], (NZ,) + g.shape), 'z', 0, 0, til...  15.9 us
  transfers between devices with their start and end apart: 51, of which 34 were waited for; matrix products, arithmetic and copies ran while one was open for 26% of the time, Pallas kernels for 0%

profile of v1, /device:TPU:8, one launch (start us, length us, event | category | flops | bytes accessed | tf_op | source)
XLA Modules:
  0.0 452.8 jit_solution(2934659408349852801)
XLA Ops:
  16.7 12.1 %all-to-all-start = ((f32[64,1,512]{2,1,0:T(1,128)}), f32[64,1,512]{2,1,0:T(1,128)S(1)}, u32[]{:S(2)}, u32[]{:S(2)}) async-start(f32[64,1,512]{2,1,0:T(1,128)} %broadcast_in_dim.11), calls=%async_computation | async-start | bytes 262144 | tf_op jit(solution)/shard_map/all_to_all | solution.py:69
  29.9 8.9 %all-to-all-done = f32[64,1,512]{2,1,0:T(1,128)S(1)} async-done(((f32[64,1,512]{2,1,0:T(1,128)}), f32[64,1,512]{2,1,0:T(1,128)S(1)}, u32[]{:S(2)}, u32[]{:S(2)}) %all-to-all-start) | async-done | bytes 131104 | tf_op jit(solution)/shard_map/all_to_all | solution.py:69
  44.5 32.5 %collective-permute-done.7 = f32[512]{0:T(512)S(1)} collective-permute-done((f32[512]{0:T(512)S(1)}, f32[512]{0:T(512)S(1)}, u32[]{:S(2)}, u32[]{:S(2)}) %collective-permute-start.7) | collective-permute-done | bytes 2080 | tf_op jit(solution)/shard_map/ppermute | solution.py:21
  97.2 9.6 %collective-permute-done.13 = bf16[1024,512]{1,0:T(8,128)(2,1)} collective-permute-done((bf16[1024,512]{1,0:T(8,128)(2,1)S(1)}, bf16[1024,512]{1,0:T(8,128)(2,1)}, u32[]{:S(2)}, u32[]{:S(2)}) %collective-permute-start.13) | collective-permute-done | bytes 1048608 | tf_op jit(solution)/shard_map/ppermute | solution.py:61
  110.3 5.4 %fusion.14 = f32[1,512,512]{2,1,0:T(8,128)S(1)} fusion(bf16[2048,512]{1,0:T(8,128)(2,1)S(1)} %multiply_convert_fusion.1, pred[]{:T(512)S(6)} %or.12, bf16[1024,512]{1,0:T(8,128)(2,1)} %collective-permute-done.13, bf16[1024,512]{1,0:T(8,128)(2,1)} %collective-permute-done.12, f32[512]{0:T(512)S(1)} %collective-permute-done.8, f32[]{:T(128)S(6)} %add.333, ...), kind=kOutput, calls=%fused_computation.34 | convolution fusion | flops 1094713344 | bytes 5253125 | tf_op jit(solution)/shard_map/dot_general | solution.py:25
  131.4 10.4 %collective-permute-done.15 = f32[4,64,512]{2,1,0:T(8,128)} collective-permute-done((f32[4,64,512]{2,1,0:T(8,128)}, f32[4,64,512]{2,1,0:T(8,128)}, u32[]{:S(2)}, u32[]{:S(2)}) %collective-permute-start.15) | collective-permute-done | bytes 524320 | tf_op jit(solution)/shard_map/ppermute | solution.py:106
  144.6 9.2 %collective-permute-done.17 = f32[4,64,512]{2,1,0:T(8,128)} collective-permute-done((f32[4,64,512]{2,1,0:T(8,128)S(1)}, f32[4,64,512]{2,1,0:T(8,128)}, u32[]{:S(2)}, u32[]{:S(2)}) %collective-permute-start.17) | collective-permute-done | bytes 524320 | tf_op jit(solution)/shard_map/ppermute | solution.py:106
  155.3 23.8 %all_to_all.31 = f32[8,4,8,512]{3,2,1,0:T(8,128)S(1)} all-to-all(f32[8,4,8,512]{3,2,1,0:T(8,128)S(1)} %copy_bitcast_fusion), channel_id=1, replica_groups=mesh['z'=8,'y'=4,'core'=2,'x'=4] {'z'}, dimensions={0} | all-to-all | bytes 1048576 | tf_op jit(solution)/shard_map/all_to_all | solution.py:109
  183.3 5.1 %collective-permute-done.19 = f32[2,8,512]{2,1,0:T(8,128)S(1)} collective-permute-done((f32[2,8,512]{2,1,0:T(8,128)S(1)}, f32[2,8,512]{2,1,0:T(8,128)S(1)}, u32[]{:S(2)}, u32[]{:S(2)}) %collective-permute-start.19) | collective-permute-done | bytes 32800 | tf_op jit(solution)/shard_map/ppermute | solution.py:110
  188.4 15.9 %all_to_all.32 = f32[8,4,8,512]{3,2,1,0:T(8,128)S(1)} all-to-all(f32[8,4,8,512]{3,2,1,0:T(8,128)S(1)} %broadcast_in_dim.14), channel_id=1, replica_groups=mesh['z'=8,'y'=4,'core'=2,'x'=4] {'z'}, dimensions={0} | all-to-all | bytes 1048576 | tf_op jit(solution)/shard_map/all_to_all | solution.py:113
  210.1 9.1 %collective-permute-done.20 = f32[8,4,8,512]{3,2,1,0:T(8,128)S(1)} collective-permute-done((f32[8,4,8,512]{3,2,1,0:T(8,128)S(1)}, f32[8,4,8,512]{3,2,1,0:T(8,128)S(1)}, u32[]{:S(2)}, u32[]{:S(2)}) %collective-permute-start.20) | collective-permute-done | bytes 524320 | tf_op jit(solution)/shard_map/ppermute | solution.py:114
  219.2 6.2 %collective-permute-done.21 = f32[8,4,8,512]{3,2,1,0:T(8,128)S(1)} collective-permute-done((f32[8,4,8,512]{3,2,1,0:T(8,128)S(1)}, f32[8,4,8,512]{3,2,1,0:T(8,128)S(1)}, u32[]{:S(2)}, u32[]{:S(2)}) %collective-permute-start.21) | collective-permute-done | bytes 524320 | tf_op jit(solution)/shard_map/ppermute | solution.py:114
  237.1 7.2 %all-to-all-start.3 = ((f32[64,1,128]{2,1,0:T(1,128)}), f32[64,1,128]{2,1,0:T(1,128)S(1)}, u32[]{:S(2)}, u32[]{:S(2)}) async-start(f32[64,1,128]{2,1,0:T(1,128)} %bitcast.39), calls=%async_computation.3 | async-start | bytes 65536 | tf_op jit(solution)/shard_map/all_to_all | solution.py:97
  244.3 8.5 %all-to-all-done.3 = f32[64,1,128]{2,1,0:T(1,128)S(1)} async-done(((f32[64,1,128]{2,1,0:T(1,128)}), f32[64,1,128]{2,1,0:T(1,128)S(1)}, u32[]{:S(2)}, u32[]{:S(2)}) %all-to-all-start.3) | async-done | bytes 32800 | tf_op jit(solution)/shard_map/all_to_all | solution.py:97
  253.5 5.7 %all-to-all-start.4 = ((bf16[64,1,128]{2,1,0:T(2,128)(2,1)}), bf16[64,1,128]{2,1,0:T(2,128)(2,1)S(1)}, u32[]{:S(2)}, u32[]{:S(2)}) async-start(bf16[64,1,128]{2,1,0:T(2,128)(2,1)} %broadcast_in_dim.16), calls=%async_computation.4 | async-start | bytes 65536 | tf_op jit(solution)/shard_map/all_to_all | solution.py:99
  259.2 8.6 %all-to-all-done.4 = bf16[64,1,128]{2,1,0:T(2,128)(2,1)S(1)} async-done(((bf16[64,1,128]{2,1,0:T(2,128)(2,1)}), bf16[64,1,128]{2,1,0:T(2,128)(2,1)S(1)}, u32[]{:S(2)}, u32[]{:S(2)}) %all-to-all-start.4) | async-done | bytes 16416 | tf_op jit(solution)/shard_map/all_to_all | solution.py:99
  286.1 5.9 %collective-permute-done.24 = f32[64,512]{1,0:T(8,128)S(1)} collective-permute-done((f32[64,512]{1,0:T(8,128)S(1)}, f32[64,512]{1,0:T(8,128)S(1)}, u32[]{:S(2)}, u32[]{:S(2)}) %collective-permute-start.24) | collective-permute-done | bytes 131104 | tf_op jit(solution)/shard_map/ppermute | solution.py:21
  297.4 5.8 %cholesky.124 = f32[64,64]{1,0:T(8,128)S(1)} custom-call(f32[64,64]{1,0:T(8,128)S(1)} %fusion.99), custom_call_target="Cholesky" | custom-call | tf_op jit(solution)/shard_map/jit(cholesky)/cholesky | solution.py:129
  324.6 5.8 %cholesky.135 = f32[64,64]{1,0:T(8,128)S(1)} custom-call(f32[64,64]{1,0:T(8,128)S(1)} %fusion.97), custom_call_target="Cholesky" | custom-call | tf_op jit(solution)/shard_map/jit(cholesky)/cholesky | solution.py:129
  331.7 4.9 %custom-call.19 = f32[1,64,64]{1,2,0:T(8,128)S(1)} custom-call(f32[1,64,64]{2,1,0:T(8,128)S(1)} %fusion.86), custom_call_target="InvertDiagBlocksLowerTriangular" | custom-call | tf_op jit(solution)/shard_map/triangular_solve/custom-call.2 | solution.py:13
  352.6 5.8 %cholesky.146 = f32[64,64]{1,0:T(8,128)S(1)} custom-call(f32[64,64]{1,0:T(8,128)S(1)} %fusion.95), custom_call_target="Cholesky" | custom-call | tf_op jit(solution)/shard_map/jit(cholesky)/cholesky | solution.py:129
  381.1 5.8 %cholesky.157 = f32[64,64]{1,0:T(8,128)S(1)} custom-call(f32[64,64]{1,0:T(8,128)S(1)} %fusion.93), custom_call_target="Cholesky" | custom-call | tf_op jit(solution)/shard_map/jit(cholesky)/cholesky | solution.py:129
  409.5 5.8 %cholesky.168 = f32[64,64]{1,0:T(8,128)S(1)} custom-call(f32[64,64]{1,0:T(8,128)S(1)} %fusion.91), custom_call_target="Cholesky" | custom-call | tf_op jit(solution)/shard_map/jit(cholesky)/cholesky | solution.py:129
  430.7 5.1 %collective-permute-start.40 = (bf16[64,1024]{1,0:T(8,128)(2,1)S(1)}, bf16[64,1024]{1,0:T(8,128)(2,1)S(1)}, u32[]{:S(2)}, u32[]{:S(2)}) collective-permute-start(bf16[64,1024]{1,0:T(8,128)(2,1)S(1)} %get-tuple-element.28), channel_id=1, source_target_pairs={{0,2},{1,3},{2,0},{3,1},{4,6},{5,7},{6,4},{7,5},{8,10},{9,11},{10,... | collective-permute-start | bytes 393224 | tf_op jit(solution)/shard_map/ppermute | solution.py:134
  (248 shorter events, 225.3 us)
Async XLA Ops:
  4.2 24.8 %collective-permute-start.3 = (f32[4096]{0:T(1024)S(1)}, f32[4096]{0:T(1024)S(1)}, u32[]{:S(2)}, u32[]{:S(2)}) collective-permute-start(f32[4096]{0:T(1024)S(1)} %get-tuple-element.4), channel_id=1, source_target_pairs={{0,2},{1,3},{2,0},{3,1},{4,6},{5,7},{6,4},{7,5},{8,10},{9,11},{10,... | collective-permute-start | bytes 49160 | tf_op jit(solution)/shard_map/ppermute | solution.py:21
  7.3 22.6 %collective-permute-start.4 = (f32[4096]{0:T(1024)S(1)}, f32[4096]{0:T(1024)S(1)}, u32[]{:S(2)}, u32[]{:S(2)}) collective-permute-start(f32[4096]{0:T(1024)S(1)} %get-tuple-element.4), channel_id=1, source_target_pairs={{0,3},{1,0},{2,1},{3,2},{4,7},{5,4},{6,5},{7,6},{8,11},{9,8},{10,9... | collective-permute-start | bytes 49160 | tf_op jit(solution)/shard_map/ppermute | solution.py:21
  8.4 21.5 %collective-permute-start.5 = (f32[4096]{0:T(1024)S(1)}, f32[4096]{0:T(1024)S(1)}, u32[]{:S(2)}, u32[]{:S(2)}) collective-permute-start(f32[4096]{0:T(1024)S(1)} %get-tuple-element.4), channel_id=1, source_target_pairs={{0,1},{1,2},{2,3},{3,0},{4,5},{5,6},{6,7},{7,4},{8,9},{9,10},{10,1... | collective-permute-start | bytes 49160 | tf_op jit(solution)/shard_map/ppermute | solution.py:21
  13.7 79.4 %collective-permute-start.11 = (bf16[1024,512]{1,0:T(8,128)(2,1)S(1)}, bf16[1024,512]{1,0:T(8,128)(2,1)}, u32[]{:S(2)}, u32[]{:S(2)}) collective-permute-start(bf16[1024,512]{1,0:T(8,128)(2,1)S(1)} %get-tuple-element.16), channel_id=1, source_target_pairs={{0,3},{1,0},{2,1},{3,2},{4,5},{5,6},{6,7},{7,4},{8,11},{9,8},{10,9... | collective-permute-start | bytes 3145736 | tf_op jit(solution)/shard_map/ppermute | solution.py:63
  16.7 22.1 %all-to-all-start = ((f32[64,1,512]{2,1,0:T(1,128)}), f32[64,1,512]{2,1,0:T(1,128)S(1)}, u32[]{:S(2)}, u32[]{:S(2)}) async-start(f32[64,1,512]{2,1,0:T(1,128)} %broadcast_in_dim.11), calls=%async_computation | async-start | bytes 262144 | tf_op jit(solution)/shard_map/all_to_all | solution.py:69
  28.8 61.4 %collective-permute-start.10 = (bf16[1024,512]{1,0:T(8,128)(2,1)}, bf16[1024,512]{1,0:T(8,128)(2,1)}, u32[]{:S(2)}, u32[]{:S(2)}) collective-permute-start(bf16[1024,512]{1,0:T(8,128)(2,1)} %get-tuple-element.17), channel_id=1, source_target_pairs={{0,3},{1,0},{2,1},{3,2},{4,7},{5,4},{6,5},{7,6},{8,11},{9,8},{10,9... | collective-permute-start | bytes 3145736 | tf_op jit(solution)/shard_map/ppermute | solution.py:60
  29.0 61.3 %collective-permute-start.9 = (bf16[1024,512]{1,0:T(8,128)(2,1)}, bf16[1024,512]{1,0:T(8,128)(2,1)}, u32[]{:S(2)}, u32[]{:S(2)}) collective-permute-start(bf16[1024,512]{1,0:T(8,128)(2,1)} %get-tuple-element.18), channel_id=1, source_target_pairs={{0,3},{1,0},{2,1},{3,2},{4,7},{5,4},{6,5},{7,6},{8,11},{9,8},{10,9... | collective-permute-start | bytes 3145736 | tf_op jit(solution)/shard_map/ppermute | solution.py:58
  39.7 37.3 %collective-permute-start.7 = (f32[512]{0:T(512)S(1)}, f32[512]{0:T(512)S(1)}, u32[]{:S(2)}, u32[]{:S(2)}) collective-permute-start(f32[512]{0:T(512)S(1)} %get-tuple-element.6), channel_id=1, source_target_pairs={{0,3},{1,0},{2,1},{3,2},{4,7},{5,4},{6,5},{7,6},{8,11},{9,8},{10,9... | collective-permute-start | bytes 6152 | tf_op jit(solution)/shard_map/ppermute | solution.py:21
  44.5 52.8 %collective-permute-start.12 = (bf16[1024,512]{1,0:T(8,128)(2,1)S(1)}, bf16[1024,512]{1,0:T(8,128)(2,1)}, u32[]{:S(2)}, u32[]{:S(2)}) collective-permute-start(bf16[1024,512]{1,0:T(8,128)(2,1)S(1)} %get-tuple-element.20), channel_id=1, source_target_pairs={{0,1},{1,2},{2,3},{3,0},{4,5},{5,6},{6,7},{7,4},{8,9},{9,10},{10,1... | collective-permute-start | bytes 3145736 | tf_op jit(solution)/shard_map/ppermute | solution.py:59
  82.0 24.8 %collective-permute-start.13 = (bf16[1024,512]{1,0:T(8,128)(2,1)S(1)}, bf16[1024,512]{1,0:T(8,128)(2,1)}, u32[]{:S(2)}, u32[]{:S(2)}) collective-permute-start(bf16[1024,512]{1,0:T(8,128)(2,1)S(1)} %get-tuple-element.19), channel_id=1, source_target_pairs={{0,1},{1,2},{2,3},{3,0},{4,5},{5,6},{6,7},{7,4},{8,9},{9,10},{10,1... | collective-permute-start | bytes 3145736 | tf_op jit(solution)/shard_map/ppermute | solution.py:61
  126.7 15.1 %collective-permute-start.15 = (f32[4,64,512]{2,1,0:T(8,128)}, f32[4,64,512]{2,1,0:T(8,128)}, u32[]{:S(2)}, u32[]{:S(2)}) collective-permute-start(f32[4,64,512]{2,1,0:T(8,128)} %get-tuple-element.23), channel_id=1, source_target_pairs={{0,8},{8,16},{16,24},{24,0},{1,9},{9,17},{17,25},{25,1},{2,10},{10... | collective-permute-start | bytes 1572872 | tf_op jit(solution)/shard_map/ppermute | solution.py:106
  128.1 16.4 %collective-permute-start.16 = (f32[4,64,512]{2,1,0:T(8,128)S(1)}, f32[4,64,512]{2,1,0:T(8,128)}, u32[]{:S(2)}, u32[]{:S(2)}) collective-permute-start(f32[4,64,512]{2,1,0:T(8,128)S(1)} %get-tuple-element.25), channel_id=1, source_target_pairs={{0,16},{8,24},{16,0},{24,8},{1,17},{9,25},{17,1},{25,9},{2,18},{10... | collective-permute-start | bytes 1572872 | tf_op jit(solution)/shard_map/ppermute | solution.py:106
  129.0 24.8 %collective-permute-start.17 = (f32[4,64,512]{2,1,0:T(8,128)S(1)}, f32[4,64,512]{2,1,0:T(8,128)}, u32[]{:S(2)}, u32[]{:S(2)}) collective-permute-start(f32[4,64,512]{2,1,0:T(8,128)S(1)} %get-tuple-element.24), channel_id=1, source_target_pairs={{0,24},{8,0},{16,8},{24,16},{1,25},{9,1},{17,9},{25,17},{2,26},{10... | collective-permute-start | bytes 1572872 | tf_op jit(solution)/shard_map/ppermute | solution.py:106
  204.4 14.8 %collective-permute-start.20 = (f32[8,4,8,512]{3,2,1,0:T(8,128)S(1)}, f32[8,4,8,512]{3,2,1,0:T(8,128)S(1)}, u32[]{:S(2)}, u32[]{:S(2)}) collective-permute-start(f32[8,4,8,512]{3,2,1,0:T(8,128)S(1)} %all_to_all.32), channel_id=1, source_target_pairs={{0,24},{8,0},{16,8},{24,16},{1,25},{9,1},{17,9},{25,17},{2,26},{10... | collective-permute-start | bytes 1572872 | tf_op jit(solution)/shard_map/ppermute | solution.py:114
  205.3 20.1 %collective-permute-start.21 = (f32[8,4,8,512]{3,2,1,0:T(8,128)S(1)}, f32[8,4,8,512]{3,2,1,0:T(8,128)S(1)}, u32[]{:S(2)}, u32[]{:S(2)}) collective-permute-start(f32[8,4,8,512]{3,2,1,0:T(8,128)S(1)} %all_to_all.32), channel_id=1, source_target_pairs={{0,16},{8,24},{16,0},{24,8},{1,17},{9,25},{17,1},{25,9},{2,18},{10... | collective-permute-start | bytes 1572872 | tf_op jit(solution)/shard_map/ppermute | solution.py:114
  207.4 18.9 %collective-permute-start.22 = (f32[8,4,8,512]{3,2,1,0:T(8,128)S(1)}, f32[8,4,8,512]{3,2,1,0:T(8,128)S(1)}, u32[]{:S(2)}, u32[]{:S(2)}) collective-permute-start(f32[8,4,8,512]{3,2,1,0:T(8,128)S(1)} %all_to_all.32), channel_id=1, source_target_pairs={{0,8},{8,16},{16,24},{24,0},{1,9},{9,17},{17,25},{25,1},{2,10},{10... | collective-permute-start | bytes 1572872 | tf_op jit(solution)/shard_map/ppermute | solution.py:114
  228.5 45.9 %collective-permute-start.23 = (f32[4,8,4,8,512]{4,3,2,1,0:T(8,128)S(1)}, f32[4,8,4,8,512]{4,3,2,1,0:T(8,128)}, u32[]{:S(2)}, u32[]{:S(2)}) collective-permute-start(f32[4,8,4,8,512]{4,3,2,1,0:T(8,128)S(1)} %constant_dynamic-slice_fusion.3), channel_id=1, source_target_pairs={{0,4},{4,0},{1,5},{5,1},{2,6},{6,2},{3,7},{7,3},{8,12},{12,8},{9,1... | collective-permute-start | bytes 6291464 | tf_op jit(solution)/shard_map/ppermute | solution.py:115
  229.8 14.5 %collective-permute-start.1 = (bf16[64,512]{1,0:T(8,128)(2,1)S(1)}, bf16[64,512]{1,0:T(8,128)(2,1)S(1)}, u32[]{:S(2)}, u32[]{:S(2)}) collective-permute-start(bf16[64,512]{1,0:T(8,128)(2,1)S(1)} %copy-done.6), channel_id=1, source_target_pairs={{0,2},{1,3},{2,0},{3,1},{4,6},{5,7},{6,4},{7,5},{8,10},{9,11},{10,... | collective-permute-start | bytes 196616 | tf_op jit(solution)/shard_map/ppermute | solution.py:21
  230.4 28.8 %collective-permute-start.2 = (bf16[64,512]{1,0:T(8,128)(2,1)S(1)}, bf16[64,512]{1,0:T(8,128)(2,1)S(1)}, u32[]{:S(2)}, u32[]{:S(2)}) collective-permute-start(bf16[64,512]{1,0:T(8,128)(2,1)S(1)} %copy-done.6), channel_id=1, source_target_pairs={{0,1},{1,2},{2,3},{3,0},{4,5},{5,6},{6,7},{7,4},{8,9},{9,10},{10,1... | collective-permute-start | bytes 196616 | tf_op jit(solution)/shard_map/ppermute | solution.py:21
  237.1 15.7 %all-to-all-start.3 = ((f32[64,1,128]{2,1,0:T(1,128)}), f32[64,1,128]{2,1,0:T(1,128)S(1)}, u32[]{:S(2)}, u32[]{:S(2)}) async-start(f32[64,1,128]{2,1,0:T(1,128)} %bitcast.39), calls=%async_computation.3 | async-start | bytes 65536 | tf_op jit(solution)/shard_map/all_to_all | solution.py:97
  253.5 14.3 %all-to-all-start.4 = ((bf16[64,1,128]{2,1,0:T(2,128)(2,1)}), bf16[64,1,128]{2,1,0:T(2,128)(2,1)S(1)}, u32[]{:S(2)}, u32[]{:S(2)}) async-start(bf16[64,1,128]{2,1,0:T(2,128)(2,1)} %broadcast_in_dim.16), calls=%async_computation.4 | async-start | bytes 65536 | tf_op jit(solution)/shard_map/all_to_all | solution.py:99
  267.9 158.0 %collective-permute-start.45 = (bf16[16,512]{1,0:T(8,128)(2,1)S(1)}, bf16[16,512]{1,0:T(8,128)(2,1)S(1)}, u32[]{:S(2)}, u32[]{:S(2)}) collective-permute-start(bf16[16,512]{1,0:T(8,128)(2,1)S(1)} %convert_element_type.98), channel_id=1, source_target_pairs={{0,2},{1,3},{2,0},{3,1},{4,6},{5,7},{6,4},{7,5},{8,10},{9,11},{10,... | collective-permute-start | bytes 49160 | tf_op jit(solution)/shard_map/ppermute | solution.py:21
  269.3 156.7 %collective-permute-start.47 = (bf16[16,512]{1,0:T(8,128)(2,1)S(1)}, bf16[16,512]{1,0:T(8,128)(2,1)S(1)}, u32[]{:S(2)}, u32[]{:S(2)}) collective-permute-start(bf16[16,512]{1,0:T(8,128)(2,1)S(1)} %convert_element_type.98), channel_id=1, source_target_pairs={{0,1},{1,2},{2,3},{3,0},{4,5},{5,6},{6,7},{7,4},{8,9},{9,10},{10,1... | collective-permute-start | bytes 49160 | tf_op jit(solution)/shard_map/ppermute | solution.py:21
  270.9 155.3 %collective-permute-start.46 = (bf16[16,512]{1,0:T(8,128)(2,1)S(1)}, bf16[16,512]{1,0:T(8,128)(2,1)S(1)}, u32[]{:S(2)}, u32[]{:S(2)}) collective-permute-start(bf16[16,512]{1,0:T(8,128)(2,1)S(1)} %convert_element_type.98), channel_id=1, source_target_pairs={{0,3},{1,0},{2,1},{3,2},{4,7},{5,4},{6,5},{7,6},{8,11},{9,8},{10,9... | collective-permute-start | bytes 49160 | tf_op jit(solution)/shard_map/ppermute | solution.py:21
  (35 other events, 192.4 us)
